TPU v7x, 32 devices: a whole 2x2x4 slice. The times are simulated.
32 devices in a mesh: row: 8 (over y, x, core), rep: 4 (over z).
Axes of the slice: x: 2, y: 2, z: 4, core: 2. Of those that a mesh axis runs over, the one named last changes fastest.
Arguments:
- features: bfloat16 [8192, 256], P('row'), may hold values from -6 to 6
- weight_self: bfloat16 [256, 256], replicated, may hold values from -0.375 to 0.375
- weight_neigh: bfloat16 [256, 256], replicated, may hold values from -0.375 to 0.375
- degrees: int32 [8192], P('row'), may hold values from 1 to 47
- tile_values: bfloat16 [8, 8, 48, 128, 128], P('row', 'rep'), may hold values from 0 to 1
- tile_blocks: int32 [8, 8, 48, 2], P('row', 'rep'), may hold values from 0 to 7
- tile_count: int32 [8, 8], P('row', 'rep'), may hold values from 1 to 48, as said below
- cotangent: bfloat16 [8192, 256], P(('row', 'rep')), may hold values from -6 to 6
Outputs:
- output: bfloat16 [8192, 256], P(('row', 'rep'))
- grad_self: float32 [256, 256], replicated
- grad_neigh: float32 [256, 256], replicated
- grad_features: bfloat16 [8192, 256], P(('row', 'rep'))
Inputs may be any that keep to these rules, and one draw needn't show every extreme that they name: `tile_count`: for some row index and section all 48 slots are live in every draw.
All inputs are finite; a program needn't handle non-finite values.
Results may differ from a plain program's by a relative error of at most 0.024.
Values may be sent and summed in bfloat16 or wider, within the bound.
A program may use at most 64 MiB of HBM per device.

v0:
```python
import jax
import jax.numpy as jnp
from jax import lax
from jax.sharding import PartitionSpec as P


def from_root(value, axis, source):
    kept = jnp.where(lax.axis_index(axis) == source, value, 0).astype(value.dtype)
    return lax.psum(kept, axis)


def hot_tables(blocks, count, nblk, slots):
    live = (jnp.arange(slots) < count).astype(jnp.float32)
    dest_hot = (blocks[:, 0][:, None] == jnp.arange(nblk)[None, :]).astype(jnp.float32) * live[
        :, None
    ]
    src_hot = (blocks[:, 1][:, None] == jnp.arange(nblk)[None, :]).astype(jnp.float32)
    return (dest_hot, src_hot)


def body(
    features, weight_self, weight_neigh, degrees, tile_values, tile_blocks, tile_count, cotangent
):
    rows, width = features.shape
    tile = tile_values.shape[3]
    slots = tile_values.shape[2]
    sections_here = tile_values.shape[1]
    nblk = rows // tile
    nrep = lax.axis_size("rep")
    share = rows // nrep
    rep_pos = lax.axis_index("rep")
    row_pos = lax.axis_index("row")
    partial_value = jnp.zeros((nblk, tile, width), jnp.float32)
    for section in range(sections_here):
        source = from_root(features, "row", rep_pos * sections_here + section)
        source_blocks = source.reshape(nblk, tile, width)
        dest_hot, src_hot = hot_tables(tile_blocks[0, section], tile_count[0, section], nblk, slots)
        picked = jnp.einsum(
            "tc,cif->tif",
            src_hot.astype(jnp.bfloat16),
            source_blocks,
            preferred_element_type=jnp.bfloat16,
        )
        prod = jnp.einsum(
            "tij,tjf->tif", tile_values[0, section], picked, preferred_element_type=jnp.float32
        )
        partial_value = partial_value + jnp.einsum("tb,tif->bif", dest_hot, prod)
    partial_value = partial_value.reshape(rows, width)
    degree_all = degrees.astype(jnp.float32)[:, None]
    degree_mine = lax.dynamic_slice_in_dim(degree_all, rep_pos * share, share, 0)
    feat_mine = lax.dynamic_slice_in_dim(features, rep_pos * share, share, 0)
    agg_part = lax.psum_scatter(partial_value, "rep", scatter_dimension=0, tiled=True)
    agg_mine = (agg_part / degree_mine).astype(jnp.bfloat16)
    pre = jnp.dot(feat_mine, weight_self, preferred_element_type=jnp.float32) + jnp.dot(
        agg_mine, weight_neigh, preferred_element_type=jnp.float32
    )
    sig = jax.nn.sigmoid(pre)
    gpre_mine = (cotangent.astype(jnp.float32) * sig * (1.0 + pre * (1.0 - sig))).astype(
        jnp.bfloat16
    )
    dagg_mine = (
        jnp.dot(gpre_mine, weight_neigh.T, preferred_element_type=jnp.float32) / degree_mine
    ).astype(jnp.bfloat16)
    dagg_all = lax.all_gather(dagg_mine, "rep", axis=0, tiled=True)
    output = jax.nn.silu(pre).astype(jnp.bfloat16)
    grad_self_part = jnp.dot(feat_mine.T, gpre_mine, preferred_element_type=jnp.float32)
    grad_neigh_part = jnp.dot(agg_mine.T, gpre_mine, preferred_element_type=jnp.float32)
    grad_self, grad_neigh = lax.psum((grad_self_part, grad_neigh_part), ("row", "rep"))
    dagg_blocks = dagg_all.reshape(nblk, tile, width)
    terms = []
    for section in range(sections_here):
        dest_hot, src_hot = hot_tables(tile_blocks[0, section], tile_count[0, section], nblk, slots)
        picked = jnp.einsum(
            "tb,bif->tif",
            dest_hot.astype(jnp.bfloat16),
            dagg_blocks,
            preferred_element_type=jnp.bfloat16,
        )
        contrib = jnp.einsum(
            "tij,tif->tjf", tile_values[0, section], picked, preferred_element_type=jnp.float32
        )
        terms.append(jnp.einsum("tc,tjf->cjf", src_hot, contrib).reshape(rows, width))
    stacked = jnp.stack(terms, 0)
    summed = lax.psum(stacked, "row")
    owned = lax.dynamic_index_in_dim(summed, row_pos % sections_here, 0, keepdims=False).astype(
        jnp.bfloat16
    )
    everyone = from_root(owned, "rep", row_pos // sections_here)
    back_mine = lax.dynamic_slice_in_dim(everyone, rep_pos * share, share, 0)
    grad_features = (
        jnp.dot(gpre_mine, weight_self.T, preferred_element_type=jnp.float32)
        + back_mine.astype(jnp.float32)
    ).astype(jnp.bfloat16)
    return (output, grad_self, grad_neigh, grad_features)


def solution(mesh):
    in_specs = (
        P("row", None),
        P(),
        P(),
        P("row"),
        P("row", "rep", None, None, None),
        P("row", "rep", None, None),
        P("row", "rep"),
        P(("row", "rep"), None),
    )
    out_specs = (P(("row", "rep"), None), P(), P(), P(("row", "rep"), None))
    return jax.shard_map(body, mesh=mesh, in_specs=in_specs, out_specs=out_specs, check_vma=False)
```

profile of v0, /device:TPU:0, one launch (start us, length us, event | category | flops | bytes accessed | tf_op | source)
XLA Modules:
  0.0 399.4 jit_solution(14081113110862203722)
XLA Ops:
  7.2 2.3 broadcast_select_fusion.1
  9.5 0.0 reduce-scatter.2.cloned.1.call-start
  9.6 1.3 fusion.78
  10.9 0.6 compare_convert_fusion
  11.6 0.7 compare_convert_fusion.1
  12.2 0.7 slice_bitcast_fusion.1
  13.0 57.8 %all-reduce.11.cloned.1.call-done = (bf16[8,128,256]{2,1,0:T(8,128)(2,1)}, bf16[8,128,256]{2,1,0:T(8,128)(2,1)}) async-done(((bf16[8,128,256]{2,1,0:T(8,128)(2,1)}, bf16[8,128,256]{2,1,0:T(8,128)(2,1)}), (bf16[8,128,256]{2,1,0:T(8,128)(2,1)}, bf16[8,128,256]{2,1,0:T(8,128)(2,1)})) %all-reduce.11.cloned.1.call-update) | async-done | bytes 1048592 | tf_op jit(solution)/shard_map/psum | solution.py:9
  70.7 2.1 fusion.31
  72.8 3.3 fusion.12
  76.0 3.8 copy.22
  79.9 2.2 fusion.33
  82.1 3.2 fusion.14
  85.3 4.9 %copy.19 = bf16[48,256,128]{1,0,2:T(8,128)(2,1)} copy(bf16[48,256,128]{2,1,0:T(8,128)(2,1)} %fusion.14) | data formatting | bytes 6291456 | tf_op jit(solution)/shard_map/tij,tjf->tif/dot_general | solution.py:44
  90.2 0.5 fusion.4
  90.8 1.4 copy-done.1
  92.1 0.5 fusion.24
  92.7 1.3 copy.14
  94.0 0.0 all-reduce.7.cloned.1.call-start
  94.1 0.1 dynamic-slice.3
  94.2 1.1 fusion.41
  95.3 25.4 %reduce-scatter.2.cloned.1.call-done = f32[256,256]{1,0:T(8,128)} async-done(((f32[1024,256]{1,0:T(8,128)}), f32[256,256]{1,0:T(8,128)}) %reduce-scatter.2.cloned.1.call-update) | async-done | bytes 262160 | tf_op jit(solution)/shard_map/reduce_scatter | solution.py:52
  120.7 1.9 multiply_convert_fusion
  122.7 0.2 fusion.28
  122.9 16.2 %all_gather.3 = bf16[1024,256]{1,0:T(8,128)(2,1)S(1)} all-gather(bf16[256,256]{1,0:T(8,128)(2,1)S(1)} %fusion.28), channel_id=1, replica_groups=mesh['row'=8,'rep'=4] {'rep'}, dimensions={0}, use_global_device_ids=true | all-gather | bytes 655360 | tf_op jit(solution)/shard_map/all_gather | solution.py:64
  139.1 1.0 fusion.37
  140.1 2.7 fusion.35
  142.8 3.1 fusion.10
  145.9 3.8 copy.25
  149.8 0.5 fusion.2
  150.3 1.3 copy.15
  151.6 0.2 copy-done.2
  151.8 1.2 copy-done.6
  153.0 3.1 fusion.8
  156.1 3.8 copy.27
  159.9 0.5 fusion
  160.4 0.3 copy.16
  160.8 0.4 copy-done.7
  161.1 0.1 pad_maximum_fusion
  161.3 56.4 %all-reduce.12 = bf16[2,1024,256]{2,1,0:T(8,128)(2,1)S(1)} all-reduce(f32[2,1024,256]{2,1,0:T(8,128)S(1)} %pad_maximum_fusion), channel_id=1, replica_groups=mesh['row'=8,'rep'=4] {'row'}, use_global_device_ids=true, to_apply=%region_5.6 | all-reduce | flops 524288 | bytes 3145728 | tf_op jit(solution)/shard_map/psum | solution.py:84
  217.7 0.8 fusion.30
  218.5 0.0 all-reduce.9.cloned.1.call-start
  218.6 1.8 fusion.39
  220.4 2.0 fusion.77
  222.4 32.1 %all-reduce.7.cloned.1.call-done = bf16[1024,256]{1,0:T(8,128)(2,1)} async-done(((bf16[1024,256]{1,0:T(8,128)(2,1)}), bf16[1024,256]{1,0:T(8,128)(2,1)}) %all-reduce.7.cloned.1.call-update) | async-done | bytes 524304 | tf_op jit(solution)/shard_map/psum | solution.py:9
  254.5 1.8 fusion.27
  256.3 133.3 %all-reduce.9.cloned.1.call-done = (f32[256,256]{1,0:T(8,128)}, f32[256,256]{1,0:T(8,128)}) async-done(((f32[256,256]{1,0:T(8,128)}, f32[256,256]{1,0:T(8,128)}), (f32[256,256]{1,0:T(8,128)}, f32[256,256]{1,0:T(8,128)})) %all-reduce.9.cloned.1.call-update) | async-done | bytes 524304 | tf_op jit(solution)/shard_map/psum | solution.py:68
  389.6 1.7 copy.51
  391.2 1.7 copy.52
  (37 shorter events, 0.2 us)
Async XLA Ops:
  7.2 113.6 %copy-start = (bf16[256,256]{1,0:T(8,128)(2,1)S(1)}, bf16[256,256]{1,0:T(8,128)(2,1)}, u32[]{:S(2)}) copy-start(bf16[256,256]{1,0:T(8,128)(2,1)} %param.10) | copy-start | bytes 393220
  7.2 63.5 %all-reduce.11.cloned.1.call-start = ((), (), s32[]{:S(2)}) async-start(), calls=%async_computation.4 | async-start | bytes 2097152 | tf_op jit(solution)/shard_map/psum | solution.py:9
  7.2 65.5 %copy-start.3 = (bf16[1,2,48,128,128]{4,3,2,1,0:T(8,128)(2,1)S(1)}, bf16[1,2,48,128,128]{4,3,2,1,0:T(8,128)(2,1)}, u32[]{:S(2)}) copy-start(bf16[1,2,48,128,128]{4,3,2,1,0:T(8,128)(2,1)} %param.12) | copy-start | bytes 9437188
  9.5 111.2 %reduce-scatter.2.cloned.1.call-start = ((), (), s32[]{:S(2)}) async-start(), calls=%async_computation.1 | async-start | bytes 1310720 | tf_op jit(solution)/shard_map/reduce_scatter | solution.py:52
  11.6 78.7 %copy-start.10 = (bf16[48]{0:T(256)(128)(2,1)}, bf16[48]{0:T(256)(128)(2,1)S(1)}, u32[]{:S(2)}) copy-start(bf16[48]{0:T(256)(128)(2,1)S(1)} %compare_convert_fusion) | copy-start | bytes 292
  12.2 78.5 %copy-start.12 = (bf16[48]{0:T(256)(128)(2,1)}, bf16[48]{0:T(256)(128)(2,1)S(1)}, u32[]{:S(2)}) copy-start(bf16[48]{0:T(256)(128)(2,1)S(1)} %compare_convert_fusion.1) | copy-start | bytes 292
  79.9 2.2 copy-start.4
  90.2 1.9 copy-start.1
  92.1 1.9 copy-start.9
  92.1 2.1 copy-start.8
  92.7 28.1 %copy-start.16 = (bf16[256,256]{1,0:T(8,128)(2,1)S(1)}, bf16[256,256]{1,0:T(8,128)(2,1)}, u32[]{:S(2)}) copy-start(bf16[256,256]{1,0:T(8,128)(2,1)} %param.15) | copy-start | bytes 393220
  94.0 45.1 %copy-start.13 = (bf16[48]{0:T(256)(128)(2,1)S(1)}, bf16[48]{0:T(256)(128)(2,1)}, u32[]{:S(2)}) copy-start(bf16[48]{0:T(256)(128)(2,1)} %copy-done.12) | copy-start | bytes 292
  94.0 160.5 %all-reduce.7.cloned.1.call-start = ((), (), s32[]{:S(2)}) async-start(), calls=%async_computation.2 | async-start | bytes 1048576 | tf_op jit(solution)/shard_map/psum | solution.py:9
  94.2 45.9 %copy-start.14 = (f32[256]{0:T(256)}, f32[256]{0:T(256)S(1)}, u32[]{:S(2)}) copy-start(f32[256]{0:T(256)S(1)} %dynamic-slice.3) | copy-start | bytes 3076
  122.7 17.5 %copy-start.11 = (bf16[48]{0:T(256)(128)(2,1)S(1)}, bf16[48]{0:T(256)(128)(2,1)}, u32[]{:S(2)}) copy-start(bf16[48]{0:T(256)(128)(2,1)} %copy-done.10) | copy-start | bytes 292
  139.1 3.7 copy-start.5
  149.8 2.1 copy-start.2
  149.8 3.2 copy-start.6
  159.9 1.2 copy-start.7
  161.3 59.1 %copy-start.15 = (f32[256]{0:T(256)S(1)}, f32[256]{0:T(256)}, u32[]{:S(2)}) copy-start(f32[256]{0:T(256)} %copy-done.14) | copy-start | bytes 3076
  218.5 171.0 %all-reduce.9.cloned.1.call-start = ((), (), s32[]{:S(2)}) async-start(), calls=%async_computation.3 | async-start | bytes 1048576 | tf_op jit(solution)/shard_map/psum | solution.py:68
Sparse Core Ops, SparseCore 0:
  11.2 59.4 all-reduce.10
  94.1 26.5 reduce-scatter.1
  218.7 35.8 all-reduce.6
  260.4 129.1 all-reduce.8
where the time goes:
time: 400 us; the launch traced here: 399 us
  waiting for transfers between devices  249 us (62%)
  blocking collectives  72.6 us (18%)
  matrix products  31.5 us (8%)
  local copies, waits for them, and re-layouts  28 us (7%)
  between operations  14 us (4%)
  other arithmetic  4.54 us (1%)
    psum x1, waiting for transfers between devices, body(): lax.psum((grad_self_part, grad_neigh_part), ('row', 'rep'))  133 us
    psum x2, waiting for transfers between devices, from_root(): return lax.psum(kept, axis)  89.8 us
    psum x1, blocking collectives, body(): summed = lax.psum(stacked, 'row')  56.4 us
    reduce_scatter x1, waiting for transfers between devices, body(): lax.psum_scatter(partial_value, 'rep', scatter_dimension=0, tiled=True)  25.4 us
    all_gather x1, blocking collectives, body(): dagg_all = lax.all_gather(dagg_mine, 'rep', axis=0, tiled=True)  16.2 us
    dot_general x2, local copies, waits for them, and re-layouts, body(): jnp.einsum('tij,tjf->tif', tile_values[0, section], picked, preferred_ele...  8.77 us
  transfers between devices with their start and end apart: 4, of which 4 were waited for; matrix products, arithmetic and copies ran while one was open for 3% of the time, Pallas kernels for 0%

commit v1 on v0

--- a/solution.py
+++ b/solution.py
@@ -4,9 +4,14 @@
 from jax.sharding import PartitionSpec as P
 
 
+def _push_node(mine_x, link_axis):
+    moved = jnp.sum(lax.all_gather(mine_x, link_axis), axis=0)
+    return moved
+
+
 def from_root(value, axis, source):
     kept = jnp.where(lax.axis_index(axis) == source, value, 0).astype(value.dtype)
-    return lax.psum(kept, axis)
+    return _push_node(kept, axis)
 
 
 def hot_tables(blocks, count, nblk, slots):

time: 400 us -> 419 us (1.048)
  other arithmetic: 4.54 us -> 14.2 us
  waiting for transfers between devices: 249 us -> 258 us
    all_gather x0 -> x3, waiting for transfers between devices: none -> 100 us  [_push_node(): moved = jnp.sum(lax.all_gather(mine_x, link_axis), axis=0)]
    psum x2 -> x0, waiting for transfers between devices: 89.8 us -> none  [from_root(): return lax.psum(kept, axis)]
    reduce_sum x0 -> x3, other arithmetic: none -> 9.75 us  [_push_node(): moved = jnp.sum(lax.all_gather(mine_x, link_axis), axis=0)]
  transfers between devices with their start and end apart: 4 -> 5, of which waited for: 4 -> 5; matrix products, arithmetic and copies ran while one was open for 3% -> 6% of each run, Pallas kernels for 0% -> 0%
where the time goes in v1:
time: 419 us; the launch traced here: 418 us
  waiting for transfers between devices  258 us (62%)
  blocking collectives  72.2 us (17%)
  matrix products  30.6 us (7%)
  local copies, waits for them, and re-layouts  28.1 us (7%)
  other arithmetic  14.2 us (3%)
  between operations  14.1 us (3%)
    psum x1, waiting for transfers between devices, body(): lax.psum((grad_self_part, grad_neigh_part), ('row', 'rep'))  131 us
    all_gather x3, waiting for transfers between devices, _push_node(): moved = jnp.sum(lax.all_gather(mine_x, link_axis), axis=0)  100 us
    psum x1, blocking collectives, body(): summed = lax.psum(stacked, 'row')  56 us
    reduce_scatter x1, waiting for transfers between devices, body(): lax.psum_scatter(partial_value, 'rep', scatter_dimension=0, tiled=True)  26.2 us
    all_gather x1, blocking collectives, body(): dagg_all = lax.all_gather(dagg_mine, 'rep', axis=0, tiled=True)  16.2 us
    reduce_sum x3, other arithmetic, _push_node(): moved = jnp.sum(lax.all_gather(mine_x, link_axis), axis=0)  9.75 us
    dot_general x2, local copies, waits for them, and re-layouts, body(): jnp.einsum('tij,tjf->tif', tile_values[0, section], picked, preferred_ele...  8.82 us
  transfers between devices with their start and end apart: 5, of which 5 were waited for; matrix products, arithmetic and copies ran while one was open for 6% of the time, Pallas kernels for 0%

profile of v1, /device:TPU:0, one launch (start us, length us, event | category | flops | bytes accessed | tf_op | source)
XLA Modules:
  0.0 417.7 jit_solution(13043994204881829861)
XLA Ops:
  7.2 2.2 broadcast_select_fusion
  9.5 0.7 all-gather.10.cloned.1.call-update
  10.2 1.3 fusion.81
  11.6 0.6 compare_convert_fusion.1
  12.2 0.7 compare_convert_fusion
  12.9 0.7 slice_bitcast_fusion
  13.6 35.6 %all-gather.8.cloned.1.call-done = bf16[8192,256]{1,0:T(8,128)(2,1)} async-done(((bf16[1024,256]{1,0:T(8,128)(2,1)}), bf16[8192,256]{1,0:T(8,128)(2,1)}) %all-gather.8.cloned.1.call-update) | async-done | bytes 4194320 | tf_op jit(solution)/shard_map/all_gather | solution.py:8
  49.2 3.9 reduce_sum.36
  53.1 2.1 fusion.33
  55.1 3.3 fusion.8
  58.5 3.9 copy.30
  62.3 25.4 %all-gather.10.cloned.1.call-done = bf16[8192,256]{1,0:T(8,128)(2,1)} async-done(((bf16[1024,256]{1,0:T(8,128)(2,1)}), bf16[8192,256]{1,0:T(8,128)(2,1)}) %all-gather.10.cloned.1.call-update) | async-done | bytes 4194320 | tf_op jit(solution)/shard_map/all_gather | solution.py:8
  87.7 3.7 reduce_sum.37
  91.4 2.2 fusion.31
  93.7 3.2 fusion.11
  96.9 4.9 %copy.33 = bf16[48,128,256]{2,0,1:T(8,128)(2,1)} copy(bf16[48,128,256]{1,2,0:T(8,128)(2,1)} %fusion.11) | data formatting | bytes 6291456 | tf_op jit(solution)/shard_map/tij,tjf->tif/dot_general | solution.py:49
  101.8 0.5 fusion.43
  102.3 1.4 copy-done.2
  103.7 0.5 convolution_add_fusion
  104.2 1.3 copy.34
  105.8 1.1 fusion.41
  106.9 26.2 %reduce-scatter.2.cloned.1.call-done = f32[256,256]{1,0:T(8,128)} async-done(((f32[1024,256]{1,0:T(8,128)}), f32[256,256]{1,0:T(8,128)}) %reduce-scatter.2.cloned.1.call-update) | async-done | bytes 262160 | tf_op jit(solution)/shard_map/reduce_scatter | solution.py:57
  133.0 1.9 multiply_convert_fusion
  135.0 0.2 fusion.29
  135.2 16.2 %all_gather.23 = bf16[1024,256]{1,0:T(8,128)(2,1)S(1)} all-gather(bf16[256,256]{1,0:T(8,128)(2,1)S(1)} %fusion.29), channel_id=1, replica_groups=mesh['row'=8,'rep'=4] {'rep'}, dimensions={0}, use_global_device_ids=true | all-gather | bytes 655360 | tf_op jit(solution)/shard_map/all_gather | solution.py:69
  151.4 1.0 fusion.37
  152.4 2.7 fusion.35
  155.1 3.1 fusion.14
  158.2 3.8 copy.37
  162.1 0.5 fusion.46
  162.6 1.3 copy.38
  163.9 0.2 copy-done.3
  164.1 1.2 copy-done.7
  165.3 3.1 fusion.17
  168.4 3.8 copy.41
  172.2 0.5 fusion.48
  172.8 0.3 copy.42
  173.1 0.4 copy-done.8
  173.6 56.0 %all-reduce.5 = bf16[2,1024,256]{2,1,0:T(8,128)(2,1)S(1)} all-reduce(f32[2,1024,256]{2,1,0:T(8,128)S(1)} %pad_maximum_fusion), channel_id=1, replica_groups=mesh['row'=8,'rep'=4] {'row'}, use_global_device_ids=true, to_apply=%region_5.6 | all-reduce | flops 524288 | bytes 3145728 | tf_op jit(solution)/shard_map/psum | solution.py:89
  229.6 0.8 fusion.30
  230.5 1.8 fusion.39
  232.3 2.0 fusion.80
  234.3 39.4 %all-gather.6.cloned.1.call-done = bf16[4,1024,256]{2,1,0:T(8,128)(2,1)} async-done(((bf16[1,1024,256]{2,1,0:T(8,128)(2,1)}), bf16[4,1024,256]{2,1,0:T(8,128)(2,1)}) %all-gather.6.cloned.1.call-update) | async-done | bytes 2097168 | tf_op jit(solution)/shard_map/all_gather | solution.py:8
  273.8 2.2 reduce_sum.38
  275.9 0.9 fusion.28
  276.8 131.0 %all-reduce.4.cloned.1.call-done = (f32[256,256]{1,0:T(8,128)}, f32[256,256]{1,0:T(8,128)}) async-done(((f32[256,256]{1,0:T(8,128)}, f32[256,256]{1,0:T(8,128)}), (f32[256,256]{1,0:T(8,128)}, f32[256,256]{1,0:T(8,128)})) %all-reduce.4.cloned.1.call-update) | async-done | bytes 524304 | tf_op jit(solution)/shard_map/psum | solution.py:73
  407.9 1.7 copy.71
  409.5 1.7 copy.72
  (45 shorter events, 0.6 us)
Async XLA Ops:
  7.2 125.9 %copy-start = (bf16[256,256]{1,0:T(8,128)(2,1)S(1)}, bf16[256,256]{1,0:T(8,128)(2,1)}, u32[]{:S(2)}) copy-start(bf16[256,256]{1,0:T(8,128)(2,1)} %param.10) | copy-start | bytes 393220
  7.2 42.0 %all-gather.8.cloned.1.call-start = ((), (), s32[]{:S(2)}) async-start(), calls=%async_computation.3 | async-start | bytes 4718592 | tf_op jit(solution)/shard_map/all_gather | solution.py:8
  9.4 78.3 %all-gather.10.cloned.1.call-start = ((), (), s32[]{:S(2)}) async-start(), calls=%async_computation.4 | async-start | bytes 4718592 | tf_op jit(solution)/shard_map/all_gather | solution.py:8
  10.2 122.8 %reduce-scatter.2.cloned.1.call-start = ((), (), s32[]{:S(2)}) async-start(), calls=%async_computation.1 | async-start | bytes 1310720 | tf_op jit(solution)/shard_map/reduce_scatter | solution.py:57
  12.2 89.6 %copy-start.11 = (bf16[48]{0:T(256)(128)(2,1)}, bf16[48]{0:T(256)(128)(2,1)S(1)}, u32[]{:S(2)}) copy-start(bf16[48]{0:T(256)(128)(2,1)S(1)} %compare_convert_fusion.1) | copy-start | bytes 292
  12.9 89.5 %copy-start.13 = (bf16[48]{0:T(256)(128)(2,1)}, bf16[48]{0:T(256)(128)(2,1)S(1)}, u32[]{:S(2)}) copy-start(bf16[48]{0:T(256)(128)(2,1)S(1)} %compare_convert_fusion) | copy-start | bytes 292
  49.2 5.9 %copy-start.4 = (bf16[1,2,48,128,128]{4,3,2,1,0:T(8,128)(2,1)S(1)}, bf16[1,2,48,128,128]{4,3,2,1,0:T(8,128)(2,1)}, u32[]{:S(2)}) copy-start(bf16[1,2,48,128,128]{4,3,2,1,0:T(8,128)(2,1)} %param.12) | copy-start | bytes 9437188
  91.4 2.2 copy-start.5
  101.8 1.9 copy-start.2
  103.7 2.0 copy-start.10
  103.7 2.1 copy-start.9
  104.2 28.8 %copy-start.17 = (bf16[256,256]{1,0:T(8,128)(2,1)S(1)}, bf16[256,256]{1,0:T(8,128)(2,1)}, u32[]{:S(2)}) copy-start(bf16[256,256]{1,0:T(8,128)(2,1)} %param.15) | copy-start | bytes 393220
  105.6 45.8 %copy-start.12 = (bf16[48]{0:T(256)(128)(2,1)S(1)}, bf16[48]{0:T(256)(128)(2,1)}, u32[]{:S(2)}) copy-start(bf16[48]{0:T(256)(128)(2,1)} %copy-done.11) | copy-start | bytes 292
  105.6 168.2 %all-gather.6.cloned.1.call-start = ((), (), s32[]{:S(2)}) async-start(), calls=%async_computation.2 | async-start | bytes 2621440 | tf_op jit(solution)/shard_map/all_gather | solution.py:8
  105.8 46.6 %copy-start.15 = (f32[256]{0:T(256)}, f32[256]{0:T(256)S(1)}, u32[]{:S(2)}) copy-start(f32[256]{0:T(256)S(1)} %dynamic-slice.3) | copy-start | bytes 3076
  135.0 17.5 %copy-start.14 = (bf16[48]{0:T(256)(128)(2,1)S(1)}, bf16[48]{0:T(256)(128)(2,1)}, u32[]{:S(2)}) copy-start(bf16[48]{0:T(256)(128)(2,1)} %copy-done.13) | copy-start | bytes 292
  151.4 3.7 copy-start.6
  162.1 2.1 copy-start.3
  162.1 3.2 copy-start.7
  172.2 1.2 copy-start.8
  173.6 58.7 %copy-start.16 = (f32[256]{0:T(256)S(1)}, f32[256]{0:T(256)}, u32[]{:S(2)}) copy-start(f32[256]{0:T(256)} %copy-done.15) | copy-start | bytes 3076
  230.4 180.8 %copy-start.1 = (bf16[256,256]{1,0:T(8,128)(2,1)S(1)}, bf16[256,256]{1,0:T(8,128)(2,1)}, u32[]{:S(2)}) copy-start(bf16[256,256]{1,0:T(8,128)(2,1)} %param.10) | copy-start | bytes 393220
  230.5 177.4 %all-reduce.4.cloned.1.call-start = ((), (), s32[]{:S(2)}) async-start(), calls=%async_computation.5 | async-start | bytes 1048576 | tf_op jit(solution)/shard_map/psum | solution.py:73
Sparse Core Ops, SparseCore 0:
  9.9 39.2 all-gather.7
  51.1 36.5 all-gather.9
  105.7 27.2 reduce-scatter.1
  230.6 43.1 all-gather.5
  279.6 128.1 all-reduce.3
